TPU v7x, 256 devices: a whole 4x4x8 slice. The times are simulated.
256 devices in a mesh: dp: 8 (over z), row: 8 (over y_hi, x), col: 4 (over y_lo, core).
Axes of the slice: x: 4, y: 4 (y_hi: 2, y_lo: 2; y = y_hi * 2 + y_lo), z: 8, core: 2. Of those that a mesh axis runs over, the one named last changes fastest.
Arguments:
- inputs: bfloat16 [8, 192, 64, 512], P('dp', None, 'row', 'col'), may hold values from -16 to 16
- norm_gain: float32 [192], replicated, may hold values from 0.25 to 1.75
- w_expand: bfloat16 [192, 768], replicated, may hold values from -0.4375 to 0.4375
- kernel: float32 [768, 9], replicated, may hold values from -2 to 2
- w_squeeze: float32 [768, 48], replicated, may hold values from -1.5 to 1.5
- w_excite: float32 [48, 768], replicated, may hold values from -6 to 6
- w_project: bfloat16 [768, 192], replicated, may hold values from -0.21875 to 0.21875
- cotangent: bfloat16 [8, 192, 64, 512], P('dp', None, 'row', 'col'), may hold values from -16 to 16
Outputs:
- output: bfloat16 [8, 192, 64, 512], P('dp', None, 'row', 'col')
- grad_inputs: bfloat16 [8, 192, 64, 512], P('dp', None, 'row', 'col')
- grad_gain: float32 [192], replicated
- grad_w_expand: float32 [192, 768], replicated
- grad_kernel: float32 [768, 9], replicated
- grad_w_squeeze: float32 [768, 48], replicated
- grad_w_excite: float32 [48, 768], replicated
- grad_w_project: float32 [768, 192], replicated
All inputs are finite; a program needn't handle non-finite values.
Results may differ from a plain program's by a relative error of at most 0.0019.
Values may be sent and summed in bfloat16 or wider, within the bound.
No kernel may reach another device: no remote copies, remote signals or barrier semaphores. Data moves between devices by JAX's collectives and lax.ppermute only.
A program may use at most 64 MiB of HBM per device.

v0:
```python
import jax
import jax.numpy as jnp
from jax import lax
from jax.sharding import PartitionSpec as P

EPS = 1e-06
HIGH = lax.Precision.HIGHEST


def with_halo(shard, sides, width):
    for axis, dim in sides:
        count, length = (lax.axis_size(axis), shard.shape[dim])
        up = [(i, (i + 1) % count) for i in range(count - 1)]
        down = [(j, i) for i, j in up]
        last = lax.slice_in_dim(shard, length - width, length, axis=dim)
        leading = lax.slice_in_dim(shard, 0, width, axis=dim)
        before = lax.ppermute(last, axis, up)
        after = lax.ppermute(leading, axis, down)
        shard = jnp.concatenate([before, shard, after], axis=dim)
    return shard


def silu_slope(value):
    sig = jax.nn.sigmoid(value)
    return sig * (1.0 + value * (1.0 - sig))


def normalize(inputs, norm_gain):
    widened = inputs.astype(jnp.float32)
    inverse = lax.rsqrt(jnp.mean(widened * widened, axis=1, keepdims=True) + EPS)
    normed = widened * inverse
    scaled = (normed * norm_gain[None, :, None, None]).astype(jnp.bfloat16)
    return (normed, inverse, scaled)


def expand(scaled, w_expand):
    return jnp.einsum("bchw,ce->behw", scaled, w_expand, preferred_element_type=jnp.float32)


def depthwise(hidden_pad, kernel, out_rows, out_cols):
    total = jnp.zeros((hidden_pad.shape[0], hidden_pad.shape[1], out_rows, out_cols), jnp.float32)
    for tap in range(9):
        drow, dcol = (tap // 3, tap % 3)
        total = (
            total
            + kernel[:, tap][None, :, None, None]
            * hidden_pad[:, :, drow : drow + out_rows, dcol : dcol + out_cols]
        )
    return total


def local(inputs, norm_gain, w_expand, kernel, w_squeeze, w_excite, w_project, cotangent):
    batch, chans, rows, cols = inputs.shape
    pixels = rows * cols * lax.axis_size("row") * lax.axis_size("col")
    normed, inverse, scaled = normalize(inputs, norm_gain)
    pre = expand(scaled, w_expand)
    hidden = jax.nn.silu(pre).astype(jnp.bfloat16)
    hidden_pad = with_halo(hidden, (("row", 2), ("col", 3)), 1)
    conv = depthwise(hidden_pad, kernel, rows, cols)
    act = jax.nn.silu(conv)
    pooled = lax.psum(jnp.sum(act, axis=(2, 3)), ("row", "col")) / pixels
    squeeze_pre = jnp.dot(pooled, w_squeeze, precision=HIGH)
    squeezed = jax.nn.silu(squeeze_pre)
    excite_pre = jnp.dot(squeezed, w_excite, precision=HIGH)
    excite = jax.nn.sigmoid(excite_pre)
    gated = (act * excite[:, :, None, None]).astype(jnp.bfloat16)
    proj = jnp.einsum("behw,ec->bchw", gated, w_project, preferred_element_type=jnp.float32)
    output = (inputs.astype(jnp.float32) + proj).astype(jnp.bfloat16)
    grad_gated = jnp.einsum(
        "bchw,ec->behw", cotangent, w_project, preferred_element_type=jnp.float32
    )
    grad_project = jnp.einsum("behw,bchw->ec", gated, cotangent, preferred_element_type=jnp.float32)
    grad_excite = lax.psum(jnp.sum(grad_gated * act, axis=(2, 3)), ("row", "col"))
    grad_epre = grad_excite * excite * (1.0 - excite)
    grad_wexc = jnp.einsum("bs,be->se", squeezed, grad_epre, precision=HIGH)
    grad_spre = jnp.einsum("be,se->bs", grad_epre, w_excite, precision=HIGH) * silu_slope(
        squeeze_pre
    )
    grad_wsq = jnp.einsum("be,bs->es", pooled, grad_spre, precision=HIGH)
    grad_pooled = jnp.einsum("bs,es->be", grad_spre, w_squeeze, precision=HIGH)
    grad_act = grad_gated * excite[:, :, None, None] + (grad_pooled / pixels)[:, :, None, None]
    grad_conv = (grad_act * silu_slope(conv)).astype(jnp.bfloat16)
    grad_pad = with_halo(grad_conv, (("row", 2), ("col", 3)), 1)
    grad_hidden = jnp.zeros(pre.shape, jnp.float32)
    taps = []
    for tap in range(9):
        drow, dcol = (tap // 3, tap % 3)
        grad_hidden = (
            grad_hidden
            + kernel[:, tap][None, :, None, None]
            * grad_pad[:, :, 2 - drow : 2 - drow + rows, 2 - dcol : 2 - dcol + cols]
        )
        taps.append(
            jnp.sum(
                grad_conv.astype(jnp.float32)
                * hidden_pad[:, :, drow : drow + rows, dcol : dcol + cols].astype(jnp.float32),
                axis=(0, 2, 3),
            )
        )
    grad_kernel = jnp.stack(taps, axis=1)
    grad_pre = (grad_hidden * silu_slope(pre)).astype(jnp.bfloat16)
    grad_wexp = jnp.einsum("bchw,behw->ce", scaled, grad_pre, preferred_element_type=jnp.float32)
    grad_scaled = jnp.einsum(
        "ce,behw->bchw", w_expand, grad_pre, preferred_element_type=jnp.float32
    )
    grad_gain = jnp.sum(grad_scaled * normed, axis=(0, 2, 3))
    grad_normed = grad_scaled * norm_gain[None, :, None, None]
    grad_in = inverse * (
        grad_normed - normed * jnp.mean(grad_normed * normed, axis=1, keepdims=True)
    ) + cotangent.astype(jnp.float32)
    grad_wsq_all, grad_wexc_all = lax.psum((grad_wsq, grad_wexc), "dp")
    gain_all, wexp_all, kernel_all, project_all = lax.psum(
        (grad_gain, grad_wexp, grad_kernel, grad_project), ("dp", "row", "col")
    )
    return (
        output,
        grad_in.astype(jnp.bfloat16),
        gain_all,
        wexp_all,
        kernel_all,
        grad_wsq_all,
        grad_wexc_all,
        project_all,
    )


def solution(mesh):
    placed = (
        P("dp", None, "row", "col"),
        P(),
        P(),
        P(),
        P(),
        P(),
        P(),
        P("dp", None, "row", "col"),
    )
    return jax.shard_map(
        local,
        mesh=mesh,
        in_specs=placed,
        out_specs=(
            P("dp", None, "row", "col"),
            P("dp", None, "row", "col"),
            P(),
            P(),
            P(),
            P(),
            P(),
            P(),
        ),
        check_vma=False,
    )
```

profile of v0, /device:TPU:2, one launch (start us, length us, event | category | flops | bytes accessed | tf_op | source)
XLA Modules:
  0.0 487.3 jit_solution(15300703473995289829)
XLA Ops:
  7.2 1.1 fusion.59
  8.4 3.8 fusion.30
  12.2 3.4 collective-permute-start
  15.6 2.5 collective-permute-start.1
  18.1 2.7 collective-permute-done
  20.7 3.1 collective-permute-done.1
  23.9 0.1 pad_maximum_fusion.11
  23.9 1.3 collective-permute-start.2
  25.2 1.4 collective-permute-start.3
  26.7 0.1 slice_reduce_fusion.8
  26.8 3.5 collective-permute-done.3
  30.3 0.9 maximum_maximum_fusion
  31.3 7.2 %fusion.26 = (f32[768]{0:T(1024)S(1)}, f32[768]{0:T(1024)S(1)}, f32[1,768,8,128]{1,3,2,0:T(8,128)}, f32[768,8,128]{0,2,1:T(8,128)}) fusion(bf16[1,768,10,129]{1,3,2,0:T(8,128)(2,1)S(1)} %get-tuple-element.60, f32[768]{0:T(1024)S(1)} %get-tuple-element.41, bf16[1,768,1,128]{1,3,2,0:T(8,128)(2,1)S(1)} %collective-permute-done.1, ...), kind=kOutput, calls=%fused_computation.48 | convolution fusion | flops 329513472 | bytes 19989504 | tf_op jit(solution)/shard_map/bchw,ec->behw/dot_general | solution.py:69
  38.5 57.0 %all-reduce.2 = (f32[1,768]{1,0:T(1,128)S(1)}, f32[1,768]{1,0:T(1,128)S(1)}) all-reduce(f32[1,768]{1,0:T(1,128)S(1)} %reduce_sum.132, f32[1,768]{1,0:T(1,128)S(1)} %reduce_sum.134), channel_id=1, replica_groups=mesh['dp'=8,'row'=8,'col'=4] {'row','col'}, use_global_device_ids=true, to_apply=%region_2.3 | all-reduce | flops 1536 | bytes 12288 | tf_op jit(solution)/shard_map/psum | solution.py:61
  95.6 0.2 fusion.80
  95.8 0.2 convolution_reduce_fusion.1
  96.1 3.9 fusion.46
  100.0 1.9 convolution_bitcast_fusion.1
  102.0 0.2 fusion.51
  102.2 0.3 convolution_reduce_fusion
  102.5 0.9 copy-done.7
  103.4 5.6 %fusion.24 = (f32[768]{0:T(1024)S(1)}, f32[768]{0:T(1024)S(1)}, f32[768]{0:T(1024)S(1)}, f32[768]{0:T(1024)S(1)}, f32[768]{0:T(1024)S(1)}, /*index=5*/f32[768]{0...) fusion(bf16[1,768,10,129]{1,3,2,0:T(8,128)(2,1)S(1)} %copy-done.4, ...), kind=kLoop, calls=%fused_computation.44 | loop fusion | flops 32236800 | bytes 20874240 | tf_op jit(solution)/shard_map/reduce_sum | solution.py:94
  109.0 2.1 collective-permute-start.4
  111.1 11.1 %collective-permute-start.5 = (bf16[1,768,1,128]{1,3,2,0:T(8,128)(2,1)S(1)}, bf16[1,768,1,128]{1,3,2,0:T(8,128)(2,1)S(1)}, u32[]{:S(2)}, u32[]{:S(2)}) collective-permute-start(bf16[1,768,1,128]{1,3,2,0:T(8,128)(2,1)S(1)} %get-tuple-element.64), channel_id=1, source_target_pairs={{4,0},{8,4},{12,8},{16,12},{20,16},{24,20},{28,24},{5,1},{9,5},{13... | collective-permute-start | bytes 589832 | tf_op jit(solution)/shard_map/ppermute | solution.py:18
  122.1 0.7 broadcast_multiply_fusion.1
  122.9 1.0 collective-permute-done.4
  123.8 1.5 collective-permute-done.5
  125.3 0.1 pad_maximum_fusion.8
  125.4 1.3 collective-permute-start.6
  126.7 3.0 collective-permute-start.7
  129.7 0.7 broadcast_multiply_fusion
  130.5 1.0 copy.24
  131.6 0.2 all-reduce.7.cloned.1.call-start
  131.8 0.1 stack.39
  131.9 0.9 pad_maximum_fusion.1
  132.8 0.9 copy-done.5
  133.8 4.7 fusion.15
  138.5 1.1 copy-done.12
  139.7 1.4 fusion.43
  141.1 2.2 fusion.58
  143.3 0.2 fusion.57
  143.5 1.0 copy.25
  144.5 81.3 %all-reduce = (f32[192]{0:T(256)}, f32[768,9]{0,1:T(8,128)}) all-reduce(f32[192]{0:T(256)S(1)} %get-tuple-element.32, f32[768,9]{0,1:T(8,128)S(1)} %stack.39), channel_id=1, replica_groups=mesh['dp'=8,'row'=8,'col'=4] {'dp','row','col'}, use_global_device_ids=true, to_apply=%region_7.8 | all-reduce | flops 7104 | bytes 56832 | tf_op jit(solution)/shard_map/psum | solution.py:112
  225.8 247.7 %all-reduce.7.cloned.1.call-done = (f32[192,768]{1,0:T(8,128)}, f32[768,192]{0,1:T(8,128)}) async-done(((f32[192,768]{1,0:T(8,128)}, f32[768,192]{0,1:T(8,128)}), (f32[192,768]{1,0:T(8,128)}, f32[768,192]{0,1:T(8,128)})) %all-reduce.7.cloned.1.call-update) | async-done | bytes 1179664 | tf_op jit(solution)/shard_map/psum | solution.py:112
  473.5 1.9 copy.51
  475.4 1.6 copy.52
  477.0 1.6 copy.53
  478.6 1.9 copy.54
  (68 shorter events, 0.4 us)
Async XLA Ops:
  7.2 24.1 %copy-start = (bf16[768,192]{0,1:T(8,128)(2,1)S(1)}, bf16[768,192]{0,1:T(8,128)(2,1)}, u32[]{:S(2)}) copy-start(bf16[768,192]{0,1:T(8,128)(2,1)} %param.14) | copy-start | bytes 884740
  7.2 218.6 %all-reduce.9.cloned.1.call-start = ((), (), s32[]{:S(2)}) async-start(), calls=%async_computation.1 | async-start | bytes 589824 | tf_op jit(solution)/shard_map/psum | solution.py:111
  8.4 18.3 %copy-start.20 = (f32[768,9]{0,1:T(8,128)S(1)}, f32[768,9]{0,1:T(8,128)}, u32[]{:S(2)}) copy-start(f32[768,9]{0,1:T(8,128)} %param.11) | copy-start | bytes 82948
  12.2 8.5 %collective-permute-start = (bf16[1,768,1,128]{1,3,2,0:T(8,128)(2,1)S(1)}, bf16[1,768,1,128]{1,3,2,0:T(8,128)(2,1)S(1)}, u32[]{:S(2)}, u32[]{:S(2)}) collective-permute-start(bf16[1,768,1,128]{1,3,2,0:T(8,128)(2,1)S(1)} %get-tuple-element.65), channel_id=1, source_target_pairs={{0,4},{4,8},{8,12},{12,16},{16,20},{20,24},{24,28},{1,5},{5,9},{9,... | collective-permute-start | bytes 589832 | tf_op jit(solution)/shard_map/ppermute | solution.py:17
  15.6 8.3 %collective-permute-start.1 = (bf16[1,768,1,128]{1,3,2,0:T(8,128)(2,1)S(1)}, bf16[1,768,1,128]{1,3,2,0:T(8,128)(2,1)S(1)}, u32[]{:S(2)}, u32[]{:S(2)}) collective-permute-start(bf16[1,768,1,128]{1,3,2,0:T(8,128)(2,1)S(1)} %get-tuple-element.66), channel_id=1, source_target_pairs={{4,0},{8,4},{12,8},{16,12},{20,16},{24,20},{28,24},{5,1},{9,5},{13... | collective-permute-start | bytes 589832 | tf_op jit(solution)/shard_map/ppermute | solution.py:18
  20.7 10.5 %copy-start.8 = (bf16[1,768,1,128]{1,3,2,0:T(8,128)(2,1)}, bf16[1,768,1,128]{1,3,2,0:T(8,128)(2,1)S(1)}, u32[]{:S(2)}) copy-start(bf16[1,768,1,128]{1,3,2,0:T(8,128)(2,1)S(1)} %collective-permute-done) | copy-start | bytes 589828
  23.9 7.3 %copy-start.10 = (bf16[1,768,1,128]{1,3,2,0:T(8,128)(2,1)}, bf16[1,768,1,128]{1,3,2,0:T(8,128)(2,1)S(1)}, u32[]{:S(2)}) copy-start(bf16[1,768,1,128]{1,3,2,0:T(8,128)(2,1)S(1)} %collective-permute-done.1) | copy-start | bytes 589828
  23.9 2.8 collective-permute-start.2
  25.2 6.0 %copy-start.17 = (bf16[1,192,8,128]{3,2,1,0:T(8,128)(2,1)S(1)}, bf16[1,192,8,128]{3,2,1,0:T(8,128)(2,1)}, u32[]{:S(2)}) copy-start(bf16[1,192,8,128]{3,2,1,0:T(8,128)(2,1)} %param.15) | copy-start | bytes 1179652
  25.2 5.0 %collective-permute-start.3 = (bf16[1,768,10,1]{1,3,2,0:T(2,128)(2,1)S(1)}, bf16[1,768,10,1]{1,3,2,0:T(2,128)(2,1)S(1)}, u32[]{:S(2)}, u32[]{:S(2)}) collective-permute-start(bf16[1,768,10,1]{1,3,2,0:T(2,128)(2,1)S(1)} %get-tuple-element.62), channel_id=1, source_target_pairs={{1,0},{2,1},{3,2},{5,4},{6,5},{7,6},{9,8},{10,9},{11,10},{13,12},{... | collective-permute-start | bytes 46088 | tf_op jit(solution)/shard_map/ppermute | solution.py:18
  31.2 7.3 %copy-start.1 = (bf16[1,768,10,129]{1,3,2,0:T(8,128)(2,1)}, bf16[1,768,10,129]{1,3,2,0:T(8,128)(2,1)S(1)}, u32[]{:S(2)}) copy-start(bf16[1,768,10,129]{1,3,2,0:T(8,128)(2,1)S(1)} %get-tuple-element.59) | copy-start | bytes 5944324
  31.2 7.3 %copy-start.3 = (bf16[1,768,10,129]{1,3,2,0:T(8,128)(2,1)}, bf16[1,768,10,129]{1,3,2,0:T(8,128)(2,1)S(1)}, u32[]{:S(2)}) copy-start(bf16[1,768,10,129]{1,3,2,0:T(8,128)(2,1)S(1)} %get-tuple-element.60) | copy-start | bytes 5944324
  31.2 64.3 %copy-start.16 = (f32[768,48]{0,1:T(8,128)S(1)}, f32[768,48]{0,1:T(8,128)}, u32[]{:S(2)}) copy-start(f32[768,48]{0,1:T(8,128)} %param.12) | copy-start | bytes 442372
  31.3 64.5 %copy-start.15 = (f32[48,768]{1,0:T(8,128)S(1)}, f32[48,768]{1,0:T(8,128)}, u32[]{:S(2)}) copy-start(f32[48,768]{1,0:T(8,128)} %param.13) | copy-start | bytes 442372
  31.3 64.8 %copy-start.13 = (bf16[1,192,8,128]{3,2,1,0:T(8,128)(2,1)S(1)}, bf16[1,192,8,128]{3,2,1,0:T(8,128)(2,1)}, u32[]{:S(2)}) copy-start(bf16[1,192,8,128]{3,2,1,0:T(8,128)(2,1)} %param.8) | copy-start | bytes 1179652
  96.1 3.9 copy-start.6
  100.0 2.5 copy-start.2
  100.0 2.5 copy-start.4
  100.0 3.4 copy-start.7
  100.0 3.4 copy-start.9
  100.0 3.4 copy-start.11
  109.0 21.6 %copy-start.19 = (bf16[1,192,8,128]{3,1,2,0:T(8,128)(2,1)S(1)}, bf16[1,192,8,128]{3,1,2,0:T(8,128)(2,1)}, u32[]{:S(2)}) copy-start(bf16[1,192,8,128]{3,1,2,0:T(8,128)(2,1)} %fusion.46) | copy-start | bytes 1179652
  109.0 14.8 %collective-permute-start.4 = (bf16[1,768,1,128]{1,3,2,0:T(8,128)(2,1)S(1)}, bf16[1,768,1,128]{1,3,2,0:T(8,128)(2,1)S(1)}, u32[]{:S(2)}, u32[]{:S(2)}) collective-permute-start(bf16[1,768,1,128]{1,3,2,0:T(8,128)(2,1)S(1)} %get-tuple-element.63), channel_id=1, source_target_pairs={{0,4},{4,8},{8,12},{12,16},{16,20},{20,24},{24,28},{1,5},{5,9},{9,... | collective-permute-start | bytes 589832 | tf_op jit(solution)/shard_map/ppermute | solution.py:17
  111.1 14.2 %collective-permute-start.5 = (bf16[1,768,1,128]{1,3,2,0:T(8,128)(2,1)S(1)}, bf16[1,768,1,128]{1,3,2,0:T(8,128)(2,1)S(1)}, u32[]{:S(2)}, u32[]{:S(2)}) collective-permute-start(bf16[1,768,1,128]{1,3,2,0:T(8,128)(2,1)S(1)} %get-tuple-element.64), channel_id=1, source_target_pairs={{4,0},{8,4},{12,8},{16,12},{20,16},{24,20},{28,24},{5,1},{9,5},{13... | collective-permute-start | bytes 589832 | tf_op jit(solution)/shard_map/ppermute | solution.py:18
  125.4 6.5 %collective-permute-start.6 = (bf16[1,768,10,1]{1,3,2,0:T(2,128)(2,1)S(1)}, bf16[1,768,10,1]{1,3,2,0:T(2,128)(2,1)S(1)}, u32[]{:S(2)}, u32[]{:S(2)}) collective-permute-start(bf16[1,768,10,1]{1,3,2,0:T(2,128)(2,1)S(1)} %get-tuple-element.57), channel_id=1, source_target_pairs={{1,0},{2,1},{3,2},{5,4},{6,5},{7,6},{9,8},{10,9},{11,10},{13,12},{... | collective-permute-start | bytes 46088 | tf_op jit(solution)/shard_map/ppermute | solution.py:18
  126.7 5.2 %collective-permute-start.7 = (bf16[1,768,10,1]{1,3,2,0:T(2,128)(2,1)S(1)}, bf16[1,768,10,1]{1,3,2,0:T(2,128)(2,1)S(1)}, u32[]{:S(2)}, u32[]{:S(2)}) collective-permute-start(bf16[1,768,10,1]{1,3,2,0:T(2,128)(2,1)S(1)} %get-tuple-element.58), channel_id=1, source_target_pairs={{0,1},{1,2},{2,3},{4,5},{5,6},{6,7},{8,9},{9,10},{10,11},{12,13},{... | collective-permute-start | bytes 46088 | tf_op jit(solution)/shard_map/ppermute | solution.py:17
  131.6 341.9 %all-reduce.7.cloned.1.call-start = ((), (), s32[]{:S(2)}) async-start(), calls=%async_computation | async-start | bytes 2359296 | tf_op jit(solution)/shard_map/psum | solution.py:112
  131.9 1.9 copy-start.5
  133.8 5.9 %copy-start.14 = (bf16[1,192,8,128]{3,2,1,0:T(8,128)(2,1)S(1)}, bf16[1,192,8,128]{3,2,1,0:T(8,128)(2,1)}, u32[]{:S(2)}) copy-start(bf16[1,192,8,128]{3,2,1,0:T(8,128)(2,1)} %param.8) | copy-start | bytes 1179652
  133.8 5.9 %copy-start.21 = (f32[192]{0:T(256)S(1)}, f32[192]{0:T(256)}, u32[]{:S(2)}) copy-start(f32[192]{0:T(256)} %param.9) | copy-start | bytes 2308
  138.5 1.2 copy-start.12
  139.7 1.4 copy-start.22
  139.7 3.6 copy-start.18
Sparse Core Ops, SparseCore 0:
  131.7 75.7 all-reduce.8
  213.6 259.8 all-reduce.6
where the time goes:
time: 488 us; the launch traced here: 487 us
  waiting for transfers between devices  259 us (53%)
  blocking collectives  138 us (28%)
  starting transfers between devices  26.3 us (5%)
  matrix products  21.3 us (4%)
  other arithmetic  15.1 us (3%)
  between operations  14.5 us (3%)
  local copies, waits for them, and re-layouts  12.4 us (3%)
    psum x1, waiting for transfers between devices, local(): lax.psum((grad_gain, grad_wexp, grad_kernel, grad_project), ('dp', 'row',...  248 us
    psum x1, blocking collectives, local(): lax.psum((grad_gain, grad_wexp, grad_kernel, grad_project), ('dp', 'row',...  81.3 us
    psum x1, blocking collectives, local(): pooled = lax.psum(jnp.sum(act, axis=(2, 3)), ('row', 'col')) / pixels  57 us
    ppermute x4, starting transfers between devices, with_halo(): after = lax.ppermute(leading, axis, down)  16.2 us
    unnamed x52, local copies, waits for them, and re-layouts  12.1 us
    ppermute x4, starting transfers between devices, with_halo(): before = lax.ppermute(last, axis, up)  9.77 us
  transfers between devices with their start and end apart: 10, of which 6 were waited for; matrix products, arithmetic and copies ran while one was open for 3% of the time, Pallas kernels for 0%

commit v1 on v0

--- a/solution.py
+++ b/solution.py
@@ -110,7 +110,7 @@
     ) + cotangent.astype(jnp.float32)
     grad_wsq_all, grad_wexc_all = lax.psum((grad_wsq, grad_wexc), "dp")
     gain_all, wexp_all, kernel_all, project_all = lax.psum(
-        (grad_gain, grad_wexp, grad_kernel, grad_project), ("dp", "row", "col")
+        lax.psum((grad_gain, grad_wexp, grad_kernel, grad_project), "dp"), ("row", "col")
     )
     return (
         output,

time: 488 us -> 385 us (0.79)
  the two profiles are of different devices: /device:TPU:2 before, /device:TPU:0 now
where the time goes in v1:
time: 385 us
  blocking collectives  220 us (57%)
  waiting for transfers between devices  92.9 us (24%)
  matrix products  21 us (5%)
  other arithmetic  15.1 us (4%)
  between operations  14.5 us (4%)
  starting transfers between devices  12.7 us (3%)
  local copies, waits for them, and re-layouts  8.93 us (2%)
    psum x1, blocking collectives, local(): lax.psum(lax.psum((grad_gain, grad_wexp, grad_kernel, grad_project), 'dp'...  124 us
    psum x1, waiting for transfers between devices, local(): lax.psum((grad_gain, grad_wexp, grad_kernel, grad_project), 'dp')  76.8 us
    psum x1, blocking collectives, local(): pooled = lax.psum(jnp.sum(act, axis=(2, 3)), ('row', 'col')) / pixels  66.3 us
    psum x1, blocking collectives, local(): lax.psum((grad_gain, grad_wexp, grad_kernel, grad_project), 'dp')  29.4 us
    ppermute x4, waiting for transfers between devices, with_halo(): after = lax.ppermute(leading, axis, down)  12 us
    unnamed x40, local copies, waits for them, and re-layouts  8.69 us
  transfers between devices with their start and end apart: 10, of which 7 were waited for; matrix products, arithmetic and copies ran while one was open for 2% of the time, Pallas kernels for 0%

profile of v1, /device:TPU:0, one launch (start us, length us, event | category | flops | bytes accessed | tf_op | source)
XLA Modules:
  0.0 384.8 jit_solution(17542294181546297557)
XLA Ops:
  7.2 1.1 fusion.59
  8.4 3.8 fusion.30
  12.2 1.7 collective-permute-start
  13.9 1.3 collective-permute-start.1
  15.2 2.8 collective-permute-done
  18.1 4.1 %collective-permute-done.1 = bf16[1,768,1,128]{1,3,2,0:T(8,128)(2,1)S(1)} collective-permute-done((bf16[1,768,1,128]{1,3,2,0:T(8,128)(2,1)S(1)}, bf16[1,768,1,128]{1,3,2,0:T(8,128)(2,1)S(1)}, u32[]{:S(2)}, u32[]{:S(2)}) %collective-permute-start.1) | collective-permute-done | bytes 196640 | tf_op jit(solution)/shard_map/ppermute | solution.py:18
  22.2 0.1 pad_maximum_fusion.11
  22.3 1.3 collective-permute-start.2
  23.6 1.4 collective-permute-start.3
  25.0 0.1 slice_reduce_fusion.8
  25.1 3.5 collective-permute-done.3
  28.6 0.9 maximum_maximum_fusion
  29.6 7.1 %fusion.26 = (f32[768]{0:T(1024)S(1)}, f32[768]{0:T(1024)S(1)}, f32[1,768,8,128]{1,3,2,0:T(8,128)}, f32[768,8,128]{0,2,1:T(8,128)}) fusion(bf16[1,768,10,129]{1,3,2,0:T(8,128)(2,1)S(1)} %get-tuple-element.64, f32[768]{0:T(1024)S(1)} %get-tuple-element.41, bf16[1,768,1,128]{1,3,2,0:T(8,128)(2,1)S(1)} %collective-permute-done.1, ...), kind=kOutput, calls=%fused_computation.48 | convolution fusion | flops 329513472 | bytes 19989504 | tf_op jit(solution)/shard_map/bchw,ec->behw/dot_general | solution.py:69
  36.8 66.3 %all-reduce.1 = (f32[1,768]{1,0:T(1,128)S(1)}, f32[1,768]{1,0:T(1,128)S(1)}) all-reduce(f32[1,768]{1,0:T(1,128)S(1)} %reduce_sum.132, f32[1,768]{1,0:T(1,128)S(1)} %reduce_sum.134), channel_id=1, replica_groups=mesh['dp'=8,'row'=8,'col'=4] {'row','col'}, use_global_device_ids=true, to_apply=%region_2.3 | all-reduce | flops 1536 | bytes 12288 | tf_op jit(solution)/shard_map/psum | solution.py:61
  103.1 0.2 fusion.80
  103.3 0.2 convolution_reduce_fusion.1
  103.6 0.2 fusion.51
  103.8 0.3 convolution_reduce_fusion
  104.1 4.0 %convolution_bitcast_fusion.1 = f32[768,192]{0,1:T(8,128)} fusion(f32[768]{0:T(1024)S(1)} %get-tuple-element.72, bf16[192,8,128]{2,1,0:T(8,128)(2,1)S(1)} %bitcast.129, f32[1,768,8,128]{1,3,2,0:T(8,128)} %get-tuple-element.58), kind=kOutput, calls=%fused_computation.78 | convolution fusion | flops 306708480 | bytes 4131840 | tf_op jit(solution)/shard_map/behw,bchw->ec/dot_general | solution.py:72
  108.1 0.1 copy-done.6
  108.1 1.1 copy-done.7
  109.3 5.6 %fusion.24 = (f32[768]{0:T(1024)S(1)}, f32[768]{0:T(1024)S(1)}, f32[768]{0:T(1024)S(1)}, f32[768]{0:T(1024)S(1)}, f32[768]{0:T(1024)S(1)}, /*index=5*/f32[768]{0...) fusion(bf16[1,768,10,129]{1,3,2,0:T(8,128)(2,1)S(1)} %copy-done.4, ...), kind=kLoop, calls=%fused_computation.44 | loop fusion | flops 32236800 | bytes 20874240 | tf_op jit(solution)/shard_map/reduce_sum | solution.py:94
  114.9 1.3 collective-permute-start.4
  116.2 1.3 collective-permute-start.5
  117.5 0.7 broadcast_multiply_fusion.1
  118.2 1.1 collective-permute-done.4
  119.4 4.4 %collective-permute-done.5 = bf16[1,768,1,128]{1,3,2,0:T(8,128)(2,1)S(1)} collective-permute-done((bf16[1,768,1,128]{1,3,2,0:T(8,128)(2,1)S(1)}, bf16[1,768,1,128]{1,3,2,0:T(8,128)(2,1)S(1)}, u32[]{:S(2)}, u32[]{:S(2)}) %collective-permute-start.5) | collective-permute-done | bytes 196640 | tf_op jit(solution)/shard_map/ppermute | solution.py:18
  123.8 1.3 collective-permute-start.6
  125.1 3.0 collective-permute-start.7
  128.2 0.7 broadcast_multiply_fusion
  128.9 0.1 collective-permute-done.7
  129.0 0.9 pad_maximum_fusion.1
  129.9 0.2 copy-done.5
  130.1 4.7 %fusion.15 = bf16[1,768,8,128]{1,3,2,0:T(8,128)(2,1)S(1)} fusion(bf16[1,768,8,128]{1,3,2,0:T(8,128)(2,1)S(1)} %get-tuple-element.57, f32[8,128,768]{2,1,0:T(8,128)S(1)} %copy-done.5, bf16[1,768,10,129]{1,3,2,0:T(8,128)(2,1)S(1)} %get-tuple-element.60, bf16[1,768,1,128]{1,3,2,0:T(8,128)(2,1)S(1)} %collective-permute-done.4, ...), kind=kLoop, calls=%fused_computation.35 | loop fusion | flops 29097984 | bytes 16149504 | tf_op jit(solution)/shard_map/convert_element_type | solution.py:101
  134.9 1.3 fusion.43
  136.4 3.1 fusion.46
  139.5 1.0 copy.24
  140.5 0.1 stack.39
  140.5 76.8 %all-reduce.10.cloned.1.call-done = (f32[192,768]{1,0:T(8,128)}, f32[768,192]{0,1:T(8,128)}, f32[768,48]{0,1:T(8,128)}, f32[48,768]{1,0:T(8,128)}) async-done(((f32[192,768]{1,0:T(8,128)}, f32[768,192]{0,1:T(8,128)}, f32[768,48]{0,1:T(8,128)}, f32[48,768]{1,0:T(8,128)}), (f32[192,768]{1,0:T(8,128)}, f32[768,192]{0,1:T(8,128)}, f32[768,48]{0,1:T(8,128)}, f32[48,768]{1,0:T(8,128)})) %all-reduce.10.cloned.1.call-update) | async-done | bytes 1474576 | tf_op jit(solution)/shard_map/psum | solution.py:113
  217.3 0.8 fusion.58
  218.2 0.2 fusion.57
  218.4 1.0 copy.25
  219.4 29.4 %all-reduce.3 = (f32[192]{0:T(256)S(1)}, f32[768,9]{0,1:T(8,128)S(1)}) all-reduce(f32[192]{0:T(256)S(1)} %get-tuple-element.32, f32[768,9]{0,1:T(8,128)S(1)} %stack.39), channel_id=1, replica_groups=mesh['dp'=8,'row'=8,'col'=4] {'dp'}, use_global_device_ids=true, to_apply=%region_7.8 | all-reduce | flops 7104 | bytes 56832 | tf_op jit(solution)/shard_map/psum | solution.py:113
  248.9 123.9 %all-reduce = (f32[192]{0:T(256)}, f32[768,9]{0,1:T(8,128)}) all-reduce(f32[192]{0:T(256)S(1)} %get-tuple-element.49, f32[768,9]{0,1:T(8,128)S(1)} %get-tuple-element.50), channel_id=1, replica_groups=mesh['dp'=8,'row'=8,'col'=4] {'row','col'}, use_global_device_ids=true, to_apply=%region_8.9 | all-reduce | flops 7104 | bytes 56832 | tf_op jit(solution)/shard_map/psum | solution.py:112
  372.8 1.9 copy.53
  374.7 0.7 copy.54
  375.4 0.7 copy.55
  376.0 1.9 copy.56
  (58 shorter events, 0.5 us)
Async XLA Ops:
  7.2 22.4 %copy-start = (bf16[768,192]{0,1:T(8,128)(2,1)S(1)}, bf16[768,192]{0,1:T(8,128)(2,1)}, u32[]{:S(2)}) copy-start(bf16[768,192]{0,1:T(8,128)(2,1)} %param.14) | copy-start | bytes 884740
  7.2 210.1 %all-reduce.10.cloned.1.call-start = ((), (), s32[]{:S(2)}) async-start(), calls=%async_computation.1 | async-start | bytes 2949120 | tf_op jit(solution)/shard_map/psum | solution.py:113
  8.4 16.6 %copy-start.14 = (f32[768,9]{0,1:T(8,128)S(1)}, f32[768,9]{0,1:T(8,128)}, u32[]{:S(2)}) copy-start(f32[768,9]{0,1:T(8,128)} %param.11) | copy-start | bytes 82948
  12.2 5.8 %collective-permute-start = (bf16[1,768,1,128]{1,3,2,0:T(8,128)(2,1)S(1)}, bf16[1,768,1,128]{1,3,2,0:T(8,128)(2,1)S(1)}, u32[]{:S(2)}, u32[]{:S(2)}) collective-permute-start(bf16[1,768,1,128]{1,3,2,0:T(8,128)(2,1)S(1)} %get-tuple-element.69), channel_id=1, source_target_pairs={{0,4},{4,8},{8,12},{12,16},{16,20},{20,24},{24,28},{1,5},{5,9},{9,... | collective-permute-start | bytes 589832 | tf_op jit(solution)/shard_map/ppermute | solution.py:17
  13.9 8.3 %collective-permute-start.1 = (bf16[1,768,1,128]{1,3,2,0:T(8,128)(2,1)S(1)}, bf16[1,768,1,128]{1,3,2,0:T(8,128)(2,1)S(1)}, u32[]{:S(2)}, u32[]{:S(2)}) collective-permute-start(bf16[1,768,1,128]{1,3,2,0:T(8,128)(2,1)S(1)} %get-tuple-element.70), channel_id=1, source_target_pairs={{4,0},{8,4},{12,8},{16,12},{20,16},{24,20},{28,24},{5,1},{9,5},{13... | collective-permute-start | bytes 589832 | tf_op jit(solution)/shard_map/ppermute | solution.py:18
  22.3 2.8 collective-permute-start.2
  23.6 6.0 %copy-start.11 = (bf16[1,192,8,128]{3,2,1,0:T(8,128)(2,1)S(1)}, bf16[1,192,8,128]{3,2,1,0:T(8,128)(2,1)}, u32[]{:S(2)}) copy-start(bf16[1,192,8,128]{3,2,1,0:T(8,128)(2,1)} %param.15) | copy-start | bytes 1179652
  23.6 5.0 %collective-permute-start.3 = (bf16[1,768,10,1]{1,3,2,0:T(2,128)(2,1)S(1)}, bf16[1,768,10,1]{1,3,2,0:T(2,128)(2,1)S(1)}, u32[]{:S(2)}, u32[]{:S(2)}) collective-permute-start(bf16[1,768,10,1]{1,3,2,0:T(2,128)(2,1)S(1)} %get-tuple-element.66), channel_id=1, source_target_pairs={{1,0},{2,1},{3,2},{5,4},{6,5},{7,6},{9,8},{10,9},{11,10},{13,12},{... | collective-permute-start | bytes 46088 | tf_op jit(solution)/shard_map/ppermute | solution.py:18
  29.5 7.2 %copy-start.1 = (bf16[1,768,10,129]{1,3,2,0:T(8,128)(2,1)}, bf16[1,768,10,129]{1,3,2,0:T(8,128)(2,1)S(1)}, u32[]{:S(2)}) copy-start(bf16[1,768,10,129]{1,3,2,0:T(8,128)(2,1)S(1)} %get-tuple-element.63) | copy-start | bytes 5944324
  29.5 7.2 %copy-start.3 = (bf16[1,768,10,129]{1,3,2,0:T(8,128)(2,1)}, bf16[1,768,10,129]{1,3,2,0:T(8,128)(2,1)S(1)}, u32[]{:S(2)}) copy-start(bf16[1,768,10,129]{1,3,2,0:T(8,128)(2,1)S(1)} %get-tuple-element.64) | copy-start | bytes 5944324
  29.6 73.5 %copy-start.10 = (f32[768,48]{0,1:T(8,128)S(1)}, f32[768,48]{0,1:T(8,128)}, u32[]{:S(2)}) copy-start(f32[768,48]{0,1:T(8,128)} %param.12) | copy-start | bytes 442372
  29.6 73.7 %copy-start.9 = (f32[48,768]{1,0:T(8,128)S(1)}, f32[48,768]{1,0:T(8,128)}, u32[]{:S(2)}) copy-start(f32[48,768]{1,0:T(8,128)} %param.13) | copy-start | bytes 442372
  104.0 4.0 %copy-start.2 = (bf16[1,768,10,129]{1,3,2,0:T(8,128)(2,1)S(1)}, bf16[1,768,10,129]{1,3,2,0:T(8,128)(2,1)}, u32[]{:S(2)}) copy-start(bf16[1,768,10,129]{1,3,2,0:T(8,128)(2,1)} %copy-done.1) | copy-start | bytes 5944324
  104.1 4.0 %copy-start.4 = (bf16[1,768,10,129]{1,3,2,0:T(8,128)(2,1)S(1)}, bf16[1,768,10,129]{1,3,2,0:T(8,128)(2,1)}, u32[]{:S(2)}) copy-start(bf16[1,768,10,129]{1,3,2,0:T(8,128)(2,1)} %copy-done.3) | copy-start | bytes 5944324
  104.1 4.1 %copy-start.6 = (f32[1,768,8,128]{1,3,2,0:T(8,128)S(1)}, f32[1,768,8,128]{1,3,2,0:T(8,128)}, u32[]{:S(2)}) copy-start(f32[1,768,8,128]{1,3,2,0:T(8,128)} %get-tuple-element.58) | copy-start | bytes 9437188
  104.1 5.2 %copy-start.7 = (f32[768,8,128]{0,2,1:T(8,128)S(1)}, f32[768,8,128]{0,2,1:T(8,128)}, u32[]{:S(2)}) copy-start(f32[768,8,128]{0,2,1:T(8,128)} %get-tuple-element.75) | copy-start | bytes 9437188
  114.9 4.5 %collective-permute-start.4 = (bf16[1,768,1,128]{1,3,2,0:T(8,128)(2,1)S(1)}, bf16[1,768,1,128]{1,3,2,0:T(8,128)(2,1)S(1)}, u32[]{:S(2)}, u32[]{:S(2)}) collective-permute-start(bf16[1,768,1,128]{1,3,2,0:T(8,128)(2,1)S(1)} %get-tuple-element.67), channel_id=1, source_target_pairs={{0,4},{4,8},{8,12},{12,16},{16,20},{20,24},{24,28},{1,5},{5,9},{9,... | collective-permute-start | bytes 589832 | tf_op jit(solution)/shard_map/ppermute | solution.py:17
  116.2 7.6 %collective-permute-start.5 = (bf16[1,768,1,128]{1,3,2,0:T(8,128)(2,1)S(1)}, bf16[1,768,1,128]{1,3,2,0:T(8,128)(2,1)S(1)}, u32[]{:S(2)}, u32[]{:S(2)}) collective-permute-start(bf16[1,768,1,128]{1,3,2,0:T(8,128)(2,1)S(1)} %get-tuple-element.68), channel_id=1, source_target_pairs={{4,0},{8,4},{12,8},{16,12},{20,16},{24,20},{28,24},{5,1},{9,5},{13... | collective-permute-start | bytes 589832 | tf_op jit(solution)/shard_map/ppermute | solution.py:18
  123.8 5.1 %collective-permute-start.6 = (bf16[1,768,10,1]{1,3,2,0:T(2,128)(2,1)S(1)}, bf16[1,768,10,1]{1,3,2,0:T(2,128)(2,1)S(1)}, u32[]{:S(2)}, u32[]{:S(2)}) collective-permute-start(bf16[1,768,10,1]{1,3,2,0:T(2,128)(2,1)S(1)} %get-tuple-element.61), channel_id=1, source_target_pairs={{1,0},{2,1},{3,2},{5,4},{6,5},{7,6},{9,8},{10,9},{11,10},{13,12},{... | collective-permute-start | bytes 46088 | tf_op jit(solution)/shard_map/ppermute | solution.py:18
  125.1 3.9 %collective-permute-start.7 = (bf16[1,768,10,1]{1,3,2,0:T(2,128)(2,1)S(1)}, bf16[1,768,10,1]{1,3,2,0:T(2,128)(2,1)S(1)}, u32[]{:S(2)}, u32[]{:S(2)}) collective-permute-start(bf16[1,768,10,1]{1,3,2,0:T(2,128)(2,1)S(1)} %get-tuple-element.62), channel_id=1, source_target_pairs={{0,1},{1,2},{2,3},{4,5},{5,6},{6,7},{8,9},{9,10},{10,11},{12,13},{... | collective-permute-start | bytes 46088 | tf_op jit(solution)/shard_map/ppermute | solution.py:17
  128.2 1.9 copy-start.5
  130.1 4.7 %copy-start.8 = (bf16[1,192,8,128]{3,2,1,0:T(8,128)(2,1)S(1)}, bf16[1,192,8,128]{3,2,1,0:T(8,128)(2,1)}, u32[]{:S(2)}) copy-start(bf16[1,192,8,128]{3,2,1,0:T(8,128)(2,1)} %param.8) | copy-start | bytes 1179652
  130.1 4.8 %copy-start.15 = (f32[192]{0:T(256)S(1)}, f32[192]{0:T(256)}, u32[]{:S(2)}) copy-start(f32[192]{0:T(256)} %param.9) | copy-start | bytes 2308
  136.2 236.5 %all-reduce.8.cloned.1.call-start = ((), (), s32[]{:S(2)}) async-start(), calls=%async_computation | async-start | bytes 2359296 | tf_op jit(solution)/shard_map/psum | solution.py:112
  136.4 80.9 %copy-start.16 = (bf16[192,768]{1,0:T(8,128)(2,1)S(1)}, bf16[192,768]{1,0:T(8,128)(2,1)}, u32[]{:S(2)}) copy-start(bf16[192,768]{1,0:T(8,128)(2,1)} %param.10) | copy-start | bytes 884740
  217.3 157.4 %copy-start.13 = (f32[768,48]{0,1:T(8,128)S(1)}, f32[768,48]{0,1:T(8,128)}, u32[]{:S(2)}) copy-start(f32[768,48]{0,1:T(8,128)} %get-tuple-element.84) | copy-start | bytes 442372
  217.3 158.0 %copy-start.12 = (f32[48,768]{1,0:T(8,128)S(1)}, f32[48,768]{1,0:T(8,128)}, u32[]{:S(2)}) copy-start(f32[48,768]{1,0:T(8,128)} %get-tuple-element.85) | copy-start | bytes 442372
Sparse Core Ops, SparseCore 0:
  136.3 80.8 all-reduce.9
  220.6 114.2 all-reduce.7
